TPU v7x, 32 devices: a whole 2x2x4 slice. The times are simulated.
32 devices in a mesh: groups: 2 (over x), req: 16 (over z, y, core).
Axes of the slice: x: 2, y: 2, z: 4, core: 2. Of those that a mesh axis runs over, the one named last changes fastest.
Arguments:
- queries: bfloat16 [2, 2048, 512], P(None, ('groups', 'req')), parts along dimension 1, may hold values from -40 to 40
- new_kv: bfloat16 [2, 2048, 128], P(None, ('groups', 'req')), parts along dimension 1, may hold values from -4 to 4
- cache: bfloat16 [2, 2048, 128, 128], P(None, ('groups', 'req')), parts along dimension 1, may hold values from -4 to 4
- lengths: int32 [2, 256], P(None, 'groups'), parts along dimension 1, may hold values from 2 to 128
- residual: bfloat16 [2, 256, 2880], P(None, ('groups', 'req')), parts along dimension 1, may hold values from -30 to 30
- o_proj: bfloat16 [4096, 2880], P('req'), may hold values from -1 to 1
- router: bfloat16 [2880, 16], replicated, may hold values from -0.109375 to 0.109375
- w_gate: bfloat16 [64, 2880, 360], P('req'), may hold values from -0.109375 to 0.109375
- w_up: bfloat16 [64, 2880, 360], P('req'), may hold values from -0.109375 to 0.109375
- w_down: bfloat16 [64, 360, 2880], P('req'), may hold values from -0.15625 to 0.15625
- routes: int32 [2, 256, 4], P(None, ('groups', 'req')), parts along dimension 1, may hold values from 0 to 15, all different within a row; in each aligned block of 8 rows (0 to 7, 8 to 15, ..., all dimensions but the last counted through in order) at most 4 rows name the same one
Outputs:
- attended: bfloat16 [2, 256, 2880], P(None, ('groups', 'req')), parts along dimension 1
- layer_out: bfloat16 [2, 256, 2880], P(None, ('groups', 'req')), parts along dimension 1
There are 2 independent parts, one for each index of `groups`. A program takes and returns all parts, laid end to end along the dimension named above; an argument that names none is the same for every part. Nothing has to cross between parts.
Inputs may be any that keep to these rules, and one draw needn't show every extreme that they name: `routes`: each row names 4 different experts; of the 8 rows of one device of one micro-batch at most 4 name any one expert, and in every draw some expert is named by exactly 4 rows of some device.
All inputs are finite; a program needn't handle non-finite values.
Results may differ from a plain program's by a relative error of at most 0.0075.
Values may be sent and summed in bfloat16 or wider, within the bound.
A program may use at most 128 MiB of HBM per device.

v0:
```python
import math
import jax
import jax.numpy as jnp
from jax import lax
from jax.sharding import PartitionSpec as P

D = 2880
HD = 64
KVH = 8
QPK = 8
WIN = 128
EXPERTS = 16
SPLIT = 4
TOPK = 4
MB = 2
REQ_DEV = 8
FFS = 360
CAP = 4


def from_partner(value, axis, stride):
    mask = 2**stride
    pairs = [(source, source ^ mask) for source in range(lax.axis_size(axis))]
    return lax.ppermute(value, axis, pairs)


def attention_rows(query_rows, new_pair, cache_rows, live_count):
    row_total = query_rows.shape[0]
    query_heads = query_rows.reshape(row_total, QPK, HD)
    factor = 1.0 / math.sqrt(HD)
    scores = (
        jnp.einsum(
            "rqd,rpd->rqp", query_heads, cache_rows[:, :, :HD], preferred_element_type=jnp.float32
        )
        * factor
    )
    own_score = (
        jnp.einsum("rqd,rd->rq", query_heads, new_pair[:, :HD], preferred_element_type=jnp.float32)
        * factor
    )
    live = jnp.arange(WIN)[None, None, :] < live_count[:, None, None]
    masked = jnp.where(live, scores, -jnp.inf)
    top_score = jnp.maximum(jnp.max(masked, axis=2), own_score)
    weight_cached = jnp.exp(masked - top_score[:, :, None])
    weight_own = jnp.exp(own_score - top_score)
    total = jnp.sum(weight_cached, axis=2) + weight_own
    prob_cached = (weight_cached / total[:, :, None]).astype(jnp.bfloat16)
    prob_own = (weight_own / total).astype(jnp.bfloat16)
    mixed = jnp.einsum(
        "rqp,rpd->rqd", prob_cached, cache_rows[:, :, HD:], preferred_element_type=jnp.float32
    )
    mixed = (
        mixed
        + prob_own.astype(jnp.float32)[:, :, None]
        * new_pair[:, HD:].astype(jnp.float32)[:, None, :]
    )
    return mixed.astype(jnp.bfloat16)


def bit_value(device_index, bit_number):
    return device_index // (1 << bit_number) % 2


def expert_grouped(buffer, w_gate, w_up, w_down, device_count, device_index):
    batch_width = buffer.shape[0]
    spread = max(1, device_count // EXPERTS)
    experts_local = max(1, EXPERTS // device_count)
    quarters_local = SPLIT // spread
    piece_rows = CAP // spread
    sent = buffer.reshape(batch_width, EXPERTS * spread, piece_rows, D)
    arrived = lax.all_to_all(sent, "req", split_axis=1, concat_axis=2, tiled=True)
    spread_levels = spread.bit_length() - 1
    for section_bit in range(spread_levels):
        upper = bit_value(device_index, section_bit) == 1
        received = from_partner(arrived, "req", section_bit)
        arrived = jnp.where(
            upper,
            jnp.concatenate([received, arrived], axis=2),
            jnp.concatenate([arrived, received], axis=2),
        )
    gate_local = w_gate.reshape(experts_local, quarters_local, D, FFS)
    up_local = w_up.reshape(experts_local, quarters_local, D, FFS)
    down_local = w_down.reshape(experts_local, quarters_local, FFS, D)
    gate_hidden = jnp.einsum(
        "merd,eqdf->meqrf", arrived, gate_local, preferred_element_type=jnp.float32
    )
    up_hidden = jnp.einsum(
        "merd,eqdf->meqrf", arrived, up_local, preferred_element_type=jnp.float32
    )
    active = ((up_hidden + 1.0) * gate_hidden * jax.nn.sigmoid(1.702 * gate_hidden)).astype(
        jnp.bfloat16
    )
    partial_out = jnp.einsum(
        "meqrf,eqfd->merd", active, down_local, preferred_element_type=jnp.float32
    )
    for section_bit in reversed(range(spread_levels)):
        upper = bit_value(device_index, section_bit) == 1
        halves = partial_out.reshape(batch_width, experts_local, 2, partial_out.shape[2] // 2, D)
        keep_part = jnp.where(upper, halves[:, :, 1], halves[:, :, 0])
        send_part = jnp.where(upper, halves[:, :, 0], halves[:, :, 1])
        received = from_partner(send_part.astype(jnp.bfloat16), "req", section_bit).astype(
            send_part.dtype
        )
        partial_out = keep_part + received
    came_back = lax.all_to_all(
        partial_out.astype(jnp.bfloat16), "req", split_axis=2, concat_axis=1, tiled=True
    ).astype(partial_out.dtype)
    return came_back.reshape(batch_width, EXPERTS * CAP, D)


def shards(queries, new_kv, cache, lengths, residual, o_proj, router, w_gate, w_up, w_down, routes):
    device_count = lax.axis_size("req")
    device_index = lax.axis_index("req")
    group_size = device_count // KVH
    group_bits = group_size.bit_length() - 1
    local_rows = queries.shape[1]
    request_count = local_rows * group_size
    block_index = device_index % group_size
    local_lengths = lax.dynamic_slice_in_dim(lengths, block_index * local_rows, local_rows, 1)

    def process_batches(first_batch, batch_width):
        query_part = queries[first_batch : first_batch + batch_width].reshape(
            batch_width * local_rows, QPK * HD
        )
        pair_part = new_kv[first_batch : first_batch + batch_width].reshape(
            batch_width * local_rows, 2 * HD
        )
        cache_part = cache[first_batch : first_batch + batch_width].reshape(
            batch_width * local_rows, WIN, 2 * HD
        )
        live_part = local_lengths[first_batch : first_batch + batch_width].reshape(
            batch_width * local_rows
        )
        mixed = attention_rows(query_part, pair_part, cache_part, live_part)
        held = mixed.reshape(batch_width, local_rows, group_size, QPK // group_size * HD)
        for section_bit in range(group_bits):
            upper = bit_value(device_index, section_bit) == 1
            paired = held.reshape(batch_width, held.shape[1], held.shape[2] // 2, 2, held.shape[3])
            keep_part = jnp.where(upper, paired[:, :, :, 1], paired[:, :, :, 0])
            send_part = jnp.where(upper, paired[:, :, :, 0], paired[:, :, :, 1])
            received = from_partner(send_part, "req", section_bit)
            held = jnp.where(
                upper,
                jnp.concatenate([received, keep_part], axis=1),
                jnp.concatenate([keep_part, received], axis=1),
            )
        head_rows = held.reshape(batch_width, request_count, held.shape[3]).transpose(1, 0, 2)
        summed = lax.psum_scatter(
            jnp.einsum("rmk,kd->rmd", head_rows, o_proj, preferred_element_type=jnp.float32),
            "req",
            scatter_dimension=0,
            tiled=True,
        )
        attended_wide = residual[first_batch : first_batch + batch_width].astype(
            jnp.float32
        ) + summed.transpose(1, 0, 2)
        attended = attended_wide.astype(jnp.bfloat16)
        attended_wide = attended.astype(jnp.float32)
        normed = (
            attended_wide
            * lax.rsqrt(jnp.mean(attended_wide * attended_wide, axis=2, keepdims=True) + 1e-05)
        ).astype(jnp.bfloat16)
        logits = jnp.einsum("mrd,de->mre", normed, router, preferred_element_type=jnp.float32)
        route_ids = routes[first_batch : first_batch + batch_width]
        chosen = jnp.take_along_axis(logits, route_ids, axis=2)
        gates = 1.0 / jnp.sum(jnp.exp(chosen[:, :, None, :] - chosen[:, :, :, None]), axis=3)
        one_hot = (
            route_ids.reshape(batch_width, REQ_DEV * TOPK)[:, :, None]
            == jnp.arange(EXPERTS, dtype=jnp.int32)[None, None, :]
        ).astype(jnp.int32)
        earlier = jnp.cumsum(one_hot, axis=1) - one_hot
        ranks = jnp.sum(earlier * one_hot, axis=2).reshape(batch_width, REQ_DEV, TOPK)
        batch_offset = (jnp.arange(batch_width, dtype=jnp.int32) * (EXPERTS * CAP))[:, None, None]
        flat_index = batch_offset + route_ids * CAP + ranks
        repeated = jnp.repeat(normed.reshape(batch_width * REQ_DEV, D), TOPK, axis=0)
        buffer = (
            jnp.zeros((batch_width * EXPERTS * CAP, D), jnp.bfloat16)
            .at[flat_index.reshape(-1)]
            .set(repeated)
        )
        buffer = buffer.reshape(batch_width, EXPERTS, CAP, D)
        returned = expert_grouped(buffer, w_gate, w_up, w_down, device_count, device_index)
        picked = jnp.take(returned.reshape(batch_width * EXPERTS * CAP, D), flat_index, axis=0)
        mixture = jnp.sum(gates[:, :, :, None] * picked, axis=2)
        layer = (attended_wide + mixture).astype(jnp.bfloat16)
        return (attended, layer)

    results = [process_batches(batch_index, 1) for batch_index in range(MB)]
    attended_all = jnp.concatenate([result[0] for result in results], axis=0)
    layer_all = jnp.concatenate([result[1] for result in results], axis=0)
    return (attended_all, layer_all)


def solution(mesh):
    placed = (
        P(None, ("groups", "req"), None),
        P(None, ("groups", "req"), None),
        P(None, ("groups", "req"), None, None),
        P(None, "groups"),
        P(None, ("groups", "req"), None),
        P("req", None),
        P(),
        P("req", None, None),
        P("req", None, None),
        P("req", None, None),
        P(None, ("groups", "req"), None),
    )
    return jax.shard_map(
        shards,
        mesh=mesh,
        in_specs=placed,
        out_specs=(P(None, ("groups", "req"), None), P(None, ("groups", "req"), None)),
        check_vma=False,
    )
```

profile of v0, /device:TPU:0, one launch (start us, length us, event | category | flops | bytes accessed | tf_op | source)
XLA Modules:
  0.0 243.5 jit_solution(3754402669353376935)
XLA Ops:
  7.2 4.8 %fusion.88 = (bf16[1,64,128,128]{3,2,1,0:T(8,128)(2,1)}, bf16[1,64,128,128]{3,2,1,0:T(8,128)(2,1)}) fusion(bf16[2,64,128,128]{3,2,1,0:T(8,128)(2,1)} %param.17), kind=kLoop, calls=%fused_computation.172 | loop fusion | bytes 8388608 | tf_op jit(solution)/shard_map/slice | solution.py:128
  12.1 4.1 %copy.162 = bf16[1,64,128,128]{2,3,1,0:T(8,128)(2,1)} copy(bf16[1,64,128,128]{3,2,1,0:T(8,128)(2,1)} %get-tuple-element.19) | data formatting | bytes 4194304
  16.8 1.8 fusion.93
  20.5 4.1 %copy.159 = bf16[1,64,128,128]{2,3,1,0:T(8,128)(2,1)} copy(bf16[1,64,128,128]{3,2,1,0:T(8,128)(2,1)} %get-tuple-element.18) | data formatting | bytes 4194304
  25.0 1.8 fusion.94
  29.3 3.1 %copy.132 = f32[128,1,2880]{2,1,0:T(1,128)} copy(f32[128,1,2880]{0,2,1:T(8,128)S(1)} %convolution_bitcast_fusion) | data formatting | bytes 2949120 | tf_op jit(solution)/shard_map/rmk,kd->rmd/dot_general | solution.py:149
  32.9 3.1 %copy.128 = f32[128,1,2880]{2,1,0:T(1,128)} copy(f32[128,1,2880]{0,2,1:T(8,128)S(1)} %convolution_bitcast_fusion.1) | data formatting | bytes 2949120 | tf_op jit(solution)/shard_map/rmk,kd->rmd/dot_general | solution.py:149
  39.3 102.9 %all-reduce.5.cloned.1.call-done = (f32[128,1,2880]{2,1,0:T(1,128)}, f32[128,1,2880]{2,1,0:T(1,128)}) async-done(((f32[128,1,2880]{2,1,0:T(1,128)}, f32[128,1,2880]{2,1,0:T(1,128)}), (f32[128,1,2880]{2,1,0:T(1,128)}, f32[128,1,2880]{2,1,0:T(1,128)})) %all-reduce.5.cloned.1.call-update) | async-done | bytes 2949136
  144.5 1.0 scatter_custom_fusion.1
  146.3 4.1 %all-to-all-start.2 = ((bf16[1,16,4,2880]{3,2,0,1:T(4,128)(2,1)}), bf16[1,16,4,2880]{3,2,0,1:T(4,128)(2,1)S(1)}, u32[]{:S(2)}, u32[]{:S(2)}) async-start(bf16[1,16,4,2880]{3,2,0,1:T(4,128)(2,1)} %reshape.675), calls=%async_computation.2 | async-start | bytes 753664 | tf_op jit(solution)/shard_map/all_to_all | solution.py:71
  155.3 6.9 %all-to-all-done.2 = bf16[1,16,4,2880]{3,2,0,1:T(4,128)(2,1)S(1)} async-done(((bf16[1,16,4,2880]{3,2,0,1:T(4,128)(2,1)}), bf16[1,16,4,2880]{3,2,0,1:T(4,128)(2,1)S(1)}, u32[]{:S(2)}, u32[]{:S(2)}) %all-to-all-start.2) | async-done | bytes 368672 | tf_op jit(solution)/shard_map/all_to_all | solution.py:71
  162.2 3.7 %all-to-all-start = ((bf16[1,16,4,2880]{3,2,0,1:T(4,128)(2,1)}), bf16[1,16,4,2880]{3,2,0,1:T(4,128)(2,1)S(1)}, u32[]{:S(2)}, u32[]{:S(2)}) async-start(bf16[1,16,4,2880]{3,2,0,1:T(4,128)(2,1)} %reshape.668), calls=%async_computation | async-start | bytes 753664 | tf_op jit(solution)/shard_map/all_to_all | solution.py:71
  166.2 6.1 %fusion.98 = f32[64,4,360]{2,0,1:T(8,128)S(1)} fusion(bf16[64,2880,1]{1,0,2:T(8,128)(2,1)S(1)} %reshape.787, bf16[4,2880,360]{1,2,0:T(8,128)(2,1)} %param.22), kind=kOutput, calls=%fused_computation.184 | convolution fusion | flops 530841600 | bytes 9031680 | tf_op jit(solution)/shard_map/merd,eqdf->meqrf/dot_general | solution.py:84
  172.2 9.9 %fusion.2 = bf16[1,1,64,2880]{3,2,0,1:T(8,128)(2,1)S(1)} fusion(bf16[4,360,2880]{2,1,0:T(8,128)(2,1)} %param.24, f32[64,4,360]{2,0,1:T(8,128)S(1)} %fusion.98, bf16[64,2880,1]{1,0,2:T(8,128)(2,1)S(1)} %reshape.787, bf16[4,2880,360]{1,2,0:T(8,128)(2,1)} %param.23), kind=kOutput, calls=%fused_computation.12 | convolution fusion | flops 1062604800 | bytes 17694720 | tf_op jit(solution)/shard_map/meqrf,eqfd->merd/dot_general | solution.py:93
  183.3 3.0 %reduce.8 = bf16[64,2880]{1,0:T(8,128)(2,1)S(1)} reduce(bf16[64,1,1,2880]{3,2,1,0:T(2,128)(2,1)S(1)} %bitcast.159, bf16[]{:T(256)} %broadcast.520), dimensions={1,2}, to_apply=%bitcast.153.reduce_sub_computation | reduce | bytes 737282
  186.3 1.1 reshape.797
  187.4 5.8 %all-to-all-start.3 = ((bf16[16,2,5760]{2,1,0:T(2,128)(2,1)}), bf16[16,2,5760]{2,1,0:T(2,128)(2,1)S(1)}, u32[]{:S(2)}, u32[]{:S(2)}) async-start(bf16[16,2,5760]{2,1,0:T(2,128)(2,1)} %reshape.797), calls=%async_computation.3 | async-start | bytes 737280 | tf_op jit(solution)/shard_map/all_to_all | solution.py:105
  193.4 6.1 %fusion.96 = f32[64,4,360]{2,0,1:T(8,128)S(1)} fusion(bf16[64,2880,1]{1,0,2:T(8,128)(2,1)S(1)} %reshape.785, bf16[4,2880,360]{1,2,0:T(8,128)(2,1)} %param.22), kind=kOutput, calls=%fused_computation.182 | convolution fusion | flops 530841600 | bytes 9031680 | tf_op jit(solution)/shard_map/merd,eqdf->meqrf/dot_general | solution.py:84
  199.5 9.9 %fusion.3 = bf16[1,1,64,2880]{3,2,0,1:T(8,128)(2,1)S(1)} fusion(bf16[4,360,2880]{2,1,0:T(8,128)(2,1)} %param.24, f32[64,4,360]{2,0,1:T(8,128)S(1)} %fusion.96, bf16[64,2880,1]{1,0,2:T(8,128)(2,1)S(1)} %reshape.785, bf16[4,2880,360]{1,2,0:T(8,128)(2,1)} %param.23), kind=kOutput, calls=%fused_computation.13 | convolution fusion | flops 1062604800 | bytes 17694720 | tf_op jit(solution)/shard_map/meqrf,eqfd->merd/dot_general | solution.py:93
  210.0 3.0 %reduce.9 = bf16[64,2880]{1,0:T(8,128)(2,1)S(1)} reduce(bf16[64,1,1,2880]{3,2,1,0:T(2,128)(2,1)S(1)} %bitcast.160, bf16[]{:T(256)} %broadcast.520), dimensions={1,2}, to_apply=%bitcast.154.reduce_sub_computation | reduce | bytes 737282
  213.0 1.1 reshape.799
  214.1 6.0 %all-to-all-start.1 = ((bf16[16,2,5760]{2,1,0:T(2,128)(2,1)}), bf16[16,2,5760]{2,1,0:T(2,128)(2,1)}, u32[]{:S(2)}, u32[]{:S(2)}) async-start(bf16[16,2,5760]{2,1,0:T(2,128)(2,1)} %reshape.799), calls=%async_computation.1 | async-start | bytes 737280 | tf_op jit(solution)/shard_map/all_to_all | solution.py:105
  222.0 10.0 %all-to-all-done.1 = bf16[16,2,5760]{2,1,0:T(2,128)(2,1)} async-done(((bf16[16,2,5760]{2,1,0:T(2,128)(2,1)}), bf16[16,2,5760]{2,1,0:T(2,128)(2,1)}, u32[]{:S(2)}, u32[]{:S(2)}) %all-to-all-start.1) | async-done | bytes 368672 | tf_op jit(solution)/shard_map/all_to_all | solution.py:105
  232.0 2.8 %reshape.800 = bf16[64,1,1,2880]{3,2,1,0:T(2,128)(2,1)S(1)} reshape(bf16[16,2,5760]{2,1,0:T(2,128)(2,1)} %all-to-all-done.1) | data formatting | bytes 737280
  (138 shorter events, 21.9 us)
Async XLA Ops:
  7.2 21.5 %copy-start = (bf16[256,2880]{0,1:T(8,128)(2,1)S(1)}, bf16[256,2880]{0,1:T(8,128)(2,1)}, u32[]{:S(2)}) copy-start(bf16[256,2880]{0,1:T(8,128)(2,1)} %param.20) | copy-start | bytes 4423684
  7.2 135.0 %all-reduce.5.cloned.1.call-start = ((), (), s32[]{:S(2)}) async-start(), calls=%async_computation.4 | async-start | bytes 6029312
  12.1 4.1 %copy-start.4 = (bf16[2,64,512]{2,1,0:T(8,128)(2,1)S(1)}, bf16[2,64,512]{2,1,0:T(8,128)(2,1)}, u32[]{:S(2)}) copy-start(bf16[2,64,512]{2,1,0:T(8,128)(2,1)} %param.15) | copy-start | bytes 393220
  12.1 4.3 %copy-start.8 = (s32[2,128]{1,0:T(2,128)S(1)}, s32[2,128]{1,0:T(2,128)}, u32[]{:S(2)}) copy-start(s32[2,128]{1,0:T(2,128)} %param.18) | copy-start | bytes 3076
  12.1 4.4 %copy-start.7 = (bf16[2,64,128]{2,1,0:T(8,128)(2,1)S(1)}, bf16[2,64,128]{2,1,0:T(8,128)(2,1)}, u32[]{:S(2)}) copy-start(bf16[2,64,128]{2,1,0:T(8,128)(2,1)} %param.16) | copy-start | bytes 98308
  16.4 2.6 %copy-start.1 = (bf16[1,64,128,128]{2,3,1,0:T(8,128)(2,1)S(1)}, bf16[1,64,128,128]{2,3,1,0:T(8,128)(2,1)}, u32[]{:S(2)}) copy-start(bf16[1,64,128,128]{2,3,1,0:T(8,128)(2,1)} %copy.162) | copy-start | bytes 6291460
  20.0 8.7 %collective-permute-start.1 = (bf16[1,64,1,256]{3,1,2,0:T(8,128)(2,1)S(1)}, bf16[1,64,1,256]{3,1,2,0:T(8,128)(2,1)S(1)}, u32[]{:S(2)}, u32[]{:S(2)}) collective-permute-start(bf16[1,64,1,256]{3,1,2,0:T(8,128)(2,1)S(1)} %get-tuple-element.24), channel_id=1, source_target_pairs={{0,1},{1,0},{2,3},{3,2},{4,5},{5,4},{6,7},{7,6},{8,9},{9,8},{10,11... | collective-permute-start | bytes 98312 | tf_op jit(solution)/shard_map/ppermute | solution.py:24
  24.7 2.3 copy-start.2
  26.8 1.4 copy-start.6
  28.1 4.3 %collective-permute-start = (bf16[1,64,1,256]{3,1,2,0:T(8,128)(2,1)S(1)}, bf16[1,64,1,256]{3,1,2,0:T(8,128)(2,1)S(1)}, u32[]{:S(2)}, u32[]{:S(2)}) collective-permute-start(bf16[1,64,1,256]{3,1,2,0:T(8,128)(2,1)S(1)} %get-tuple-element.20), channel_id=1, source_target_pairs={{0,1},{1,0},{2,3},{3,2},{4,5},{5,4},{6,7},{7,6},{8,9},{9,8},{10,11... | collective-permute-start | bytes 98312 | tf_op jit(solution)/shard_map/ppermute | solution.py:24
  36.0 2.0 copy-start.9
  36.0 108.1 %copy-start.5 = (bf16[2,8,2880]{2,1,0:T(8,128)(2,1)S(1)}, bf16[2,8,2880]{2,1,0:T(8,128)(2,1)}, u32[]{:S(2)}) copy-start(bf16[2,8,2880]{2,1,0:T(8,128)(2,1)} %param.19) | copy-start | bytes 276484
  36.0 114.4 %copy-start.3 = (bf16[2880,16]{0,1:T(8,128)(2,1)S(1)}, bf16[2880,16]{0,1:T(8,128)(2,1)}, u32[]{:S(2)}) copy-start(bf16[2880,16]{0,1:T(8,128)(2,1)} %param.21) | copy-start | bytes 276484
  146.3 16.0 %all-to-all-start.2 = ((bf16[1,16,4,2880]{3,2,0,1:T(4,128)(2,1)}), bf16[1,16,4,2880]{3,2,0,1:T(4,128)(2,1)S(1)}, u32[]{:S(2)}, u32[]{:S(2)}) async-start(bf16[1,16,4,2880]{3,2,0,1:T(4,128)(2,1)} %reshape.675), calls=%async_computation.2 | async-start | bytes 753664 | tf_op jit(solution)/shard_map/all_to_all | solution.py:71
  162.2 25.2 %all-to-all-start = ((bf16[1,16,4,2880]{3,2,0,1:T(4,128)(2,1)}), bf16[1,16,4,2880]{3,2,0,1:T(4,128)(2,1)S(1)}, u32[]{:S(2)}, u32[]{:S(2)}) async-start(bf16[1,16,4,2880]{3,2,0,1:T(4,128)(2,1)} %reshape.668), calls=%async_computation | async-start | bytes 753664 | tf_op jit(solution)/shard_map/all_to_all | solution.py:71
  187.4 26.7 %all-to-all-start.3 = ((bf16[16,2,5760]{2,1,0:T(2,128)(2,1)}), bf16[16,2,5760]{2,1,0:T(2,128)(2,1)S(1)}, u32[]{:S(2)}, u32[]{:S(2)}) async-start(bf16[16,2,5760]{2,1,0:T(2,128)(2,1)} %reshape.797), calls=%async_computation.3 | async-start | bytes 737280 | tf_op jit(solution)/shard_map/all_to_all | solution.py:105
  214.1 17.8 %all-to-all-start.1 = ((bf16[16,2,5760]{2,1,0:T(2,128)(2,1)}), bf16[16,2,5760]{2,1,0:T(2,128)(2,1)}, u32[]{:S(2)}, u32[]{:S(2)}) async-start(bf16[16,2,5760]{2,1,0:T(2,128)(2,1)} %reshape.799), calls=%async_computation.1 | async-start | bytes 737280 | tf_op jit(solution)/shard_map/all_to_all | solution.py:105
Sparse Core Ops, SparseCore 0:
  36.1 106.0 all-reduce.4
where the time goes:
time: 244 us
  waiting for transfers between devices  120 us (49%)
  local copies, waits for them, and re-layouts  39.3 us (16%)
  matrix products  38.8 us (16%)
  starting transfers between devices  20.4 us (8%)
  between operations  15.3 us (6%)
  other arithmetic  9.88 us (4%)
    unnamed x2, waiting for transfers between devices  103 us
    dot_general x2, matrix products, expert_grouped(): jnp.einsum('meqrf,eqfd->merd', active, down_local, preferred_element_type...  19.8 us
    unnamed x30, local copies, waits for them, and re-layouts  16.8 us
    dot_general x2, matrix products, expert_grouped(): jnp.einsum('merd,eqdf->meqrf', arrived, gate_local, preferred_element_typ...  12.1 us
    all_to_all x2, starting transfers between devices, expert_grouped(): lax.all_to_all(partial_out.astype(jnp.bfloat16), 'req', split_axis=2, con...  11.8 us
    all_to_all x2, waiting for transfers between devices, expert_grouped(): lax.all_to_all(partial_out.astype(jnp.bfloat16), 'req', split_axis=2, con...  9.97 us
    all_to_all x2, starting transfers between devices, expert_grouped(): lax.all_to_all(sent, 'req', split_axis=1, concat_axis=2, tiled=True)  7.83 us
    all_to_all x2, waiting for transfers between devices, expert_grouped(): lax.all_to_all(sent, 'req', split_axis=1, concat_axis=2, tiled=True)  6.93 us
  transfers between devices with their start and end apart: 7, of which 3 were waited for; matrix products, arithmetic and copies ran while one was open for 26% of the time, Pallas kernels for 0%

commit v1 on v0

--- a/solution.py
+++ b/solution.py
@@ -68,7 +68,10 @@
     quarters_local = SPLIT // spread
     piece_rows = CAP // spread
     sent = buffer.reshape(batch_width, EXPERTS * spread, piece_rows, D)
-    arrived = lax.all_to_all(sent, "req", split_axis=1, concat_axis=2, tiled=True)
+    arrived = jnp.concatenate(
+        lax.all_to_all(jnp.stack(jnp.split(sent, lax.axis_size("req"), axis=1)), "req", 0, 0),
+        axis=2,
+    )
     spread_levels = spread.bit_length() - 1
     for section_bit in range(spread_levels):
         upper = bit_value(device_index, section_bit) == 1

time: 244 us -> 258 us (1.057)
  local copies, waits for them, and re-layouts: 39.3 us -> 57.5 us
  waiting for transfers between devices: 120 us -> 113 us
    unnamed x30 -> x60, local copies, waits for them, and re-layouts: 16.8 us -> 35.2 us
    all_to_all x2, waiting for transfers between devices: 6.93 us -> 0.01 us  [expert_grouped(): lax.all_to_all(jnp.stack(jnp.split(sent, lax.axis_size('req'), axis=1)),...]
  transfers between devices with their start and end apart: 7 -> 7, of which waited for: 3 -> 2; matrix products, arithmetic and copies ran while one was open for 26% -> 28% of each run, Pallas kernels for 0% -> 0%
where the time goes in v1:
time: 258 us; the launch traced here: 257 us
  waiting for transfers between devices  113 us (44%)
  local copies, waits for them, and re-layouts  57.5 us (22%)
  matrix products  38.8 us (15%)
  starting transfers between devices  22.9 us (9%)
  between operations  15.3 us (6%)
  other arithmetic  9.88 us (4%)
    unnamed x2, waiting for transfers between devices  103 us
    unnamed x60, local copies, waits for them, and re-layouts  35.2 us
    dot_general x2, matrix products, expert_grouped(): jnp.einsum('meqrf,eqfd->merd', active, down_local, preferred_element_type...  19.8 us
    dot_general x2, matrix products, expert_grouped(): jnp.einsum('merd,eqdf->meqrf', arrived, gate_local, preferred_element_typ...  12.1 us
    all_to_all x2, starting transfers between devices, expert_grouped(): lax.all_to_all(partial_out.astype(jnp.bfloat16), 'req', split_axis=2, con...  12.1 us
    all_to_all x2, starting transfers between devices, expert_grouped(): lax.all_to_all(jnp.stack(jnp.split(sent, lax.axis_size('req'), axis=1)),...  10.1 us
    all_to_all x2, waiting for transfers between devices, expert_grouped(): lax.all_to_all(partial_out.astype(jnp.bfloat16), 'req', split_axis=2, con...  9.97 us
    dot_general x2, local copies, waits for them, and re-layouts, process_batches(): jnp.einsum('rmk,kd->rmd', head_rows, o_proj, preferred_element_type=jnp.f...  6.17 us
  transfers between devices with their start and end apart: 7, of which 2 were waited for; matrix products, arithmetic and copies ran while one was open for 28% of the time, Pallas kernels for 0%

profile of v1, /device:TPU:0, one launch (start us, length us, event | category | flops | bytes accessed | tf_op | source)
XLA Modules:
  0.0 257.2 jit_solution(4087532599490681514)
XLA Ops:
  7.2 4.8 %fusion.88 = (bf16[1,64,128,128]{3,2,1,0:T(8,128)(2,1)}, bf16[1,64,128,128]{3,2,1,0:T(8,128)(2,1)}) fusion(bf16[2,64,128,128]{3,2,1,0:T(8,128)(2,1)} %param.17), kind=kLoop, calls=%fused_computation.236 | loop fusion | bytes 8388608 | tf_op jit(solution)/shard_map/slice | solution.py:131
  12.1 4.1 %copy.222 = bf16[1,64,128,128]{2,3,1,0:T(8,128)(2,1)} copy(bf16[1,64,128,128]{3,2,1,0:T(8,128)(2,1)} %get-tuple-element.19) | data formatting | bytes 4194304
  16.8 1.8 fusion.93
  20.5 4.1 %copy.219 = bf16[1,64,128,128]{2,3,1,0:T(8,128)(2,1)} copy(bf16[1,64,128,128]{3,2,1,0:T(8,128)(2,1)} %get-tuple-element.18) | data formatting | bytes 4194304
  25.0 1.8 fusion.94
  29.3 3.1 %copy.192 = f32[128,1,2880]{2,1,0:T(1,128)} copy(f32[128,1,2880]{0,2,1:T(8,128)S(1)} %convolution_bitcast_fusion) | data formatting | bytes 2949120 | tf_op jit(solution)/shard_map/rmk,kd->rmd/dot_general | solution.py:152
  32.9 3.1 %copy.188 = f32[128,1,2880]{2,1,0:T(1,128)} copy(f32[128,1,2880]{0,2,1:T(8,128)S(1)} %convolution_bitcast_fusion.1) | data formatting | bytes 2949120 | tf_op jit(solution)/shard_map/rmk,kd->rmd/dot_general | solution.py:152
  39.3 102.9 %all-reduce.5.cloned.1.call-done = (f32[128,1,2880]{2,1,0:T(1,128)}, f32[128,1,2880]{2,1,0:T(1,128)}) async-done(((f32[128,1,2880]{2,1,0:T(1,128)}, f32[128,1,2880]{2,1,0:T(1,128)}), (f32[128,1,2880]{2,1,0:T(1,128)}, f32[128,1,2880]{2,1,0:T(1,128)})) %all-reduce.5.cloned.1.call-update) | async-done | bytes 2949136
  145.1 1.0 scatter_custom_fusion.1
  156.0 4.1 %all-to-all-start.2 = ((bf16[16,1,1,4,2880]{4,3,2,1,0:T(4,128)(2,1)}), bf16[16,1,1,4,2880]{4,3,2,1,0:T(4,128)(2,1)S(1)}, u32[]{:S(2)}, u32[]{:S(2)}) async-start(bf16[16,1,1,4,2880]{4,3,2,1,0:T(4,128)(2,1)} %constant_dynamic-update-slice_fusion.16), calls=%async_computation.2 | async-start | bytes 753664 | tf_op jit(solution)/shard_map/all_to_all | solution.py:72
  162.4 1.0 scatter_custom_fusion
  173.5 6.0 %all-to-all-start = ((bf16[16,1,1,4,2880]{4,3,2,1,0:T(4,128)(2,1)}), bf16[16,1,1,4,2880]{4,3,2,1,0:T(4,128)(2,1)S(1)}, u32[]{:S(2)}, u32[]{:S(2)}) async-start(bf16[16,1,1,4,2880]{4,3,2,1,0:T(4,128)(2,1)} %constant_dynamic-update-slice_fusion), calls=%async_computation | async-start | bytes 753664 | tf_op jit(solution)/shard_map/all_to_all | solution.py:72
  179.7 6.1 %fusion.98 = f32[64,4,360]{2,0,1:T(8,128)S(1)} fusion(bf16[64,2880,1]{1,0,2:T(8,128)(2,1)S(1)} %reshape.783, bf16[4,2880,360]{1,2,0:T(8,128)(2,1)} %param.22), kind=kOutput, calls=%fused_computation.248 | convolution fusion | flops 530841600 | bytes 9031680 | tf_op jit(solution)/shard_map/merd,eqdf->meqrf/dot_general | solution.py:87
  185.7 9.9 %fusion.2 = bf16[1,1,64,2880]{3,2,0,1:T(8,128)(2,1)S(1)} fusion(bf16[4,360,2880]{2,1,0:T(8,128)(2,1)} %param.24, f32[64,4,360]{2,0,1:T(8,128)S(1)} %fusion.98, bf16[64,2880,1]{1,0,2:T(8,128)(2,1)S(1)} %reshape.783, bf16[4,2880,360]{1,2,0:T(8,128)(2,1)} %param.23), kind=kOutput, calls=%fused_computation.12 | convolution fusion | flops 1062604800 | bytes 17694720 | tf_op jit(solution)/shard_map/meqrf,eqfd->merd/dot_general | solution.py:96
  196.8 3.0 %reduce.8 = bf16[64,2880]{1,0:T(8,128)(2,1)S(1)} reduce(bf16[64,1,1,2880]{3,2,1,0:T(2,128)(2,1)S(1)} %bitcast.283, bf16[]{:T(256)} %broadcast.520), dimensions={1,2}, to_apply=%bitcast.277.reduce_sub_computation | reduce | bytes 737282
  199.8 1.1 reshape.793
  200.9 6.0 %all-to-all-start.3 = ((bf16[16,2,5760]{2,1,0:T(2,128)(2,1)}), bf16[16,2,5760]{2,1,0:T(2,128)(2,1)S(1)}, u32[]{:S(2)}, u32[]{:S(2)}) async-start(bf16[16,2,5760]{2,1,0:T(2,128)(2,1)} %reshape.793), calls=%async_computation.3 | async-start | bytes 737280 | tf_op jit(solution)/shard_map/all_to_all | solution.py:108
  207.1 6.1 %fusion.96 = f32[64,4,360]{2,0,1:T(8,128)S(1)} fusion(bf16[64,2880,1]{1,0,2:T(8,128)(2,1)S(1)} %reshape.781, bf16[4,2880,360]{1,2,0:T(8,128)(2,1)} %param.22), kind=kOutput, calls=%fused_computation.246 | convolution fusion | flops 530841600 | bytes 9031680 | tf_op jit(solution)/shard_map/merd,eqdf->meqrf/dot_general | solution.py:87
  213.2 9.9 %fusion.3 = bf16[1,1,64,2880]{3,2,0,1:T(8,128)(2,1)S(1)} fusion(bf16[4,360,2880]{2,1,0:T(8,128)(2,1)} %param.24, f32[64,4,360]{2,0,1:T(8,128)S(1)} %fusion.96, bf16[64,2880,1]{1,0,2:T(8,128)(2,1)S(1)} %reshape.781, bf16[4,2880,360]{1,2,0:T(8,128)(2,1)} %param.23), kind=kOutput, calls=%fused_computation.13 | convolution fusion | flops 1062604800 | bytes 17694720 | tf_op jit(solution)/shard_map/meqrf,eqfd->merd/dot_general | solution.py:96
  223.7 3.0 %reduce.9 = bf16[64,2880]{1,0:T(8,128)(2,1)S(1)} reduce(bf16[64,1,1,2880]{3,2,1,0:T(2,128)(2,1)S(1)} %bitcast.284, bf16[]{:T(256)} %broadcast.520), dimensions={1,2}, to_apply=%bitcast.278.reduce_sub_computation | reduce | bytes 737282
  226.7 1.1 reshape.795
  227.8 6.0 %all-to-all-start.1 = ((bf16[16,2,5760]{2,1,0:T(2,128)(2,1)}), bf16[16,2,5760]{2,1,0:T(2,128)(2,1)}, u32[]{:S(2)}, u32[]{:S(2)}) async-start(bf16[16,2,5760]{2,1,0:T(2,128)(2,1)} %reshape.795), calls=%async_computation.1 | async-start | bytes 737280 | tf_op jit(solution)/shard_map/all_to_all | solution.py:108
  235.7 10.0 %all-to-all-done.1 = bf16[16,2,5760]{2,1,0:T(2,128)(2,1)} async-done(((bf16[16,2,5760]{2,1,0:T(2,128)(2,1)}), bf16[16,2,5760]{2,1,0:T(2,128)(2,1)}, u32[]{:S(2)}, u32[]{:S(2)}) %all-to-all-start.1) | async-done | bytes 368672 | tf_op jit(solution)/shard_map/all_to_all | solution.py:108
  245.7 2.8 %reshape.796 = bf16[64,1,1,2880]{3,2,1,0:T(2,128)(2,1)S(1)} reshape(bf16[16,2,5760]{2,1,0:T(2,128)(2,1)} %all-to-all-done.1) | data formatting | bytes 737280
  (170 shorter events, 39.1 us)
Async XLA Ops:
  7.2 21.5 %copy-start = (bf16[256,2880]{0,1:T(8,128)(2,1)S(1)}, bf16[256,2880]{0,1:T(8,128)(2,1)}, u32[]{:S(2)}) copy-start(bf16[256,2880]{0,1:T(8,128)(2,1)} %param.20) | copy-start | bytes 4423684
  7.2 135.0 %all-reduce.5.cloned.1.call-start = ((), (), s32[]{:S(2)}) async-start(), calls=%async_computation.4 | async-start | bytes 6029312
  12.1 4.1 %copy-start.4 = (bf16[2,64,512]{2,1,0:T(8,128)(2,1)S(1)}, bf16[2,64,512]{2,1,0:T(8,128)(2,1)}, u32[]{:S(2)}) copy-start(bf16[2,64,512]{2,1,0:T(8,128)(2,1)} %param.15) | copy-start | bytes 393220
  12.1 4.3 %copy-start.8 = (s32[2,128]{1,0:T(2,128)S(1)}, s32[2,128]{1,0:T(2,128)}, u32[]{:S(2)}) copy-start(s32[2,128]{1,0:T(2,128)} %param.18) | copy-start | bytes 3076
  12.1 4.4 %copy-start.7 = (bf16[2,64,128]{2,1,0:T(8,128)(2,1)S(1)}, bf16[2,64,128]{2,1,0:T(8,128)(2,1)}, u32[]{:S(2)}) copy-start(bf16[2,64,128]{2,1,0:T(8,128)(2,1)} %param.16) | copy-start | bytes 98308
  16.4 2.6 %copy-start.1 = (bf16[1,64,128,128]{2,3,1,0:T(8,128)(2,1)S(1)}, bf16[1,64,128,128]{2,3,1,0:T(8,128)(2,1)}, u32[]{:S(2)}) copy-start(bf16[1,64,128,128]{2,3,1,0:T(8,128)(2,1)} %copy.222) | copy-start | bytes 6291460
  20.0 8.7 %collective-permute-start.1 = (bf16[1,64,1,256]{3,1,2,0:T(8,128)(2,1)S(1)}, bf16[1,64,1,256]{3,1,2,0:T(8,128)(2,1)S(1)}, u32[]{:S(2)}, u32[]{:S(2)}) collective-permute-start(bf16[1,64,1,256]{3,1,2,0:T(8,128)(2,1)S(1)} %get-tuple-element.24), channel_id=1, source_target_pairs={{0,1},{1,0},{2,3},{3,2},{4,5},{5,4},{6,7},{7,6},{8,9},{9,8},{10,11... | collective-permute-start | bytes 98312 | tf_op jit(solution)/shard_map/ppermute | solution.py:24
  24.7 2.3 copy-start.2
  26.8 1.4 copy-start.6
  28.1 4.3 %collective-permute-start = (bf16[1,64,1,256]{3,1,2,0:T(8,128)(2,1)S(1)}, bf16[1,64,1,256]{3,1,2,0:T(8,128)(2,1)S(1)}, u32[]{:S(2)}, u32[]{:S(2)}) collective-permute-start(bf16[1,64,1,256]{3,1,2,0:T(8,128)(2,1)S(1)} %get-tuple-element.20), channel_id=1, source_target_pairs={{0,1},{1,0},{2,3},{3,2},{4,5},{5,4},{6,7},{7,6},{8,9},{9,8},{10,11... | collective-permute-start | bytes 98312 | tf_op jit(solution)/shard_map/ppermute | solution.py:24
  36.0 2.0 copy-start.9
  36.0 108.1 %copy-start.5 = (bf16[2,8,2880]{2,1,0:T(8,128)(2,1)S(1)}, bf16[2,8,2880]{2,1,0:T(8,128)(2,1)}, u32[]{:S(2)}) copy-start(bf16[2,8,2880]{2,1,0:T(8,128)(2,1)} %param.19) | copy-start | bytes 276484
  143.1 17.1 %copy-start.3 = (bf16[2880,16]{0,1:T(8,128)(2,1)S(1)}, bf16[2880,16]{0,1:T(8,128)(2,1)}, u32[]{:S(2)}) copy-start(bf16[2880,16]{0,1:T(8,128)(2,1)} %param.21) | copy-start | bytes 276484
  156.0 17.5 %all-to-all-start.2 = ((bf16[16,1,1,4,2880]{4,3,2,1,0:T(4,128)(2,1)}), bf16[16,1,1,4,2880]{4,3,2,1,0:T(4,128)(2,1)S(1)}, u32[]{:S(2)}, u32[]{:S(2)}) async-start(bf16[16,1,1,4,2880]{4,3,2,1,0:T(4,128)(2,1)} %constant_dynamic-update-slice_fusion.16), calls=%async_computation.2 | async-start | bytes 753664 | tf_op jit(solution)/shard_map/all_to_all | solution.py:72
  173.5 27.4 %all-to-all-start = ((bf16[16,1,1,4,2880]{4,3,2,1,0:T(4,128)(2,1)}), bf16[16,1,1,4,2880]{4,3,2,1,0:T(4,128)(2,1)S(1)}, u32[]{:S(2)}, u32[]{:S(2)}) async-start(bf16[16,1,1,4,2880]{4,3,2,1,0:T(4,128)(2,1)} %constant_dynamic-update-slice_fusion), calls=%async_computation | async-start | bytes 753664 | tf_op jit(solution)/shard_map/all_to_all | solution.py:72
  200.9 26.9 %all-to-all-start.3 = ((bf16[16,2,5760]{2,1,0:T(2,128)(2,1)}), bf16[16,2,5760]{2,1,0:T(2,128)(2,1)S(1)}, u32[]{:S(2)}, u32[]{:S(2)}) async-start(bf16[16,2,5760]{2,1,0:T(2,128)(2,1)} %reshape.793), calls=%async_computation.3 | async-start | bytes 737280 | tf_op jit(solution)/shard_map/all_to_all | solution.py:108
  227.8 17.8 %all-to-all-start.1 = ((bf16[16,2,5760]{2,1,0:T(2,128)(2,1)}), bf16[16,2,5760]{2,1,0:T(2,128)(2,1)}, u32[]{:S(2)}, u32[]{:S(2)}) async-start(bf16[16,2,5760]{2,1,0:T(2,128)(2,1)} %reshape.795), calls=%async_computation.1 | async-start | bytes 737280 | tf_op jit(solution)/shard_map/all_to_all | solution.py:108
Sparse Core Ops, SparseCore 0:
  36.1 106.0 all-reduce.4
